TPU v7x, 32 devices: a whole 2x2x4 slice. The times are simulated.
32 devices in a mesh: freq: 4 (over z), tm: 2 (over core), beam: 4 (over y, x).
Axes of the slice: x: 2, y: 2, z: 4, core: 2. Of those that a mesh axis runs over, the one named last changes fastest.
Arguments:
- intensity: bfloat16 [4, 4096, 512], P('beam', 'freq', 'tm'), parts along dimension 0, may hold values from -32 to 32
- delay_tables: int32 [3, 12, 2048], replicated, may hold values from 0 to 511, as said below
- box_widths: int32 [8], replicated, may hold values from 1 to 128
Outputs:
- snr: float32 [4, 1024, 8, 512], P('beam', 'freq', None, 'tm'), parts along dimension 0
There are 4 independent parts, one for each index of `beam`. A program takes and returns all parts, laid end to end along the dimension named above; an argument that names none is the same for every part. Nothing has to cross between parts.
Inputs may be any that keep to these rules, and one draw needn't show every extreme that they name: `delay_tables`: at merge level s (second index s - 1), with D_s = max(1, 2^(s-2)), entry [k, s-1, b D_s + d] belongs to band b and trial d; the trials (k = 0, 1) and the delay (k = 2) lie in 0 to D_(s-1) - 1; columns from (4096 / 2^s) D_s on are not read.
All inputs are finite; a program needn't handle non-finite values.
Results may differ from a plain program's by a relative error of at most 0.0003.
Values may be sent and summed in bfloat16 or wider, within the bound.
A program may use at most 64 MiB of HBM per device.

v0:
```python
import jax
import jax.numpy as jnp
from jax import lax
from jax.sharding import PartitionSpec as P

LEVELS = 12
WMAX = 128
EPSILON = 1e-05
BANDS = ("freq", "tm")


def band_count():
    return lax.axis_size("freq") * lax.axis_size("tm")


def swapped(block, stride):
    count = band_count()
    route = []
    for low in range(count):
        high = low | 1 << stride
        if high != low and high < count:
            route += [(low, high), (high, low)]
    return lax.ppermute(block, BANDS, route)


def trial_depth(merge_level):
    if merge_level >= 2:
        return 2 ** (merge_level - 2)
    return 1


def shift_rows(source, delays, columns, largest):
    result = source
    for bit_index in range(max(largest, 0).bit_length()):
        step_size = 1 << bit_index
        moved = jnp.concatenate(
            [result[..., step_size:], jnp.zeros_like(result[..., :step_size])], axis=-1
        )
        flag = delays >> bit_index & 1 == 1
        result = jnp.where(flag[None, :, None], moved, result)
    return result[..., :columns]


def merge_bands(current, delay_tables, merge_level, first_band):
    beam_count, bands_in, depth_in, columns = current.shape
    depth_out = trial_depth(merge_level)
    bands_out = bands_in // 2
    entries = lax.dynamic_slice_in_dim(
        delay_tables[:, merge_level - 1, :], first_band * depth_out, bands_out * depth_out, 1
    )
    band_base = jnp.arange(bands_out * depth_out, dtype=jnp.int32) // depth_out * depth_in
    lower_flat = current[:, 0::2].reshape(beam_count, bands_out * depth_in, columns)
    upper_flat = current[:, 1::2].reshape(beam_count, bands_out * depth_in, columns)
    picked = jnp.take(lower_flat, band_base + entries[0], axis=1)
    chosen = jnp.take(upper_flat, band_base + entries[1], axis=1)
    delayed = shift_rows(chosen, entries[2], columns, depth_in - 1)
    return (picked + delayed).reshape(beam_count, bands_out, depth_out, columns)


def merge_across(current, delay_tables, merge_level, cross_step, device_pos):
    beam_count, rows_held, columns = current.shape
    depth_in = rows_held * 2**cross_step
    depth_out = trial_depth(merge_level)
    group_size = 2 ** (cross_step + 1)
    position = device_pos % group_size
    upper_side = position // (group_size // 2)
    row_offset = position % (group_size // 2) * rows_held
    band_index = device_pos // group_size
    entries = lax.dynamic_slice_in_dim(
        delay_tables[:, merge_level - 1, :], band_index * depth_out, depth_out, 1
    )
    lower_local = entries[0] - row_offset
    lower_hit = (lower_local >= 0) & (lower_local < rows_held) & (upper_side == 0)
    lower_rows = jnp.take(current, jnp.clip(lower_local, 0, rows_held - 1), axis=1)
    upper_local = entries[1] - row_offset
    upper_hit = (upper_local >= 0) & (upper_local < rows_held) & (upper_side == 1)
    upper_chosen = jnp.take(current, jnp.clip(upper_local, 0, rows_held - 1), axis=1)
    upper_rows = shift_rows(upper_chosen, entries[2], columns, depth_in - 1)
    partial_value = jnp.where(lower_hit[None, :, None], lower_rows, 0.0) + jnp.where(
        upper_hit[None, :, None], upper_rows, 0.0
    )
    for bit_index in range(cross_step + 1):
        blocks = partial_value.shape[1] // rows_held
        paired = partial_value.reshape(beam_count, blocks // 2, 2, rows_held, columns)
        chosen_bit = device_pos >> bit_index & 1
        kept_rows = lax.dynamic_index_in_dim(paired, chosen_bit, 2, keepdims=False)
        given_rows = lax.dynamic_index_in_dim(paired, 1 - chosen_bit, 2, keepdims=False)
        partial_value = (kept_rows + swapped(given_rows, bit_index)).reshape(
            beam_count, blocks // 2 * rows_held, columns
        )
    return partial_value


def own_trials(current, delay_tables, device_pos):
    beam_count, bands_in, depth_in, columns = current.shape
    rows = trial_depth(LEVELS) // band_count()
    entries = lax.dynamic_slice_in_dim(delay_tables[:, LEVELS - 1, :], device_pos * rows, rows, 1)
    picked = jnp.take(current[:, 0], entries[0], axis=1)
    chosen = jnp.take(current[:, 1], entries[1], axis=1)
    delayed = shift_rows(chosen, entries[2], columns, depth_in - 1)
    return picked + delayed


def body(intensity, delay_tables, box_widths):
    time_parts = lax.axis_size("tm")
    time_pos = lax.axis_index("tm")
    device_pos = lax.axis_index("freq") * time_parts + time_pos
    block_len = intensity.shape[2]
    whole_rows = lax.all_to_all(intensity, "tm", 1, 2, tiled=True)
    beam_count, channels_held, time_total = whole_rows.shape
    local_levels = channels_held.bit_length() - 1
    current = whole_rows.astype(jnp.float32)[:, :, None, :]
    for merge_level in range(1, local_levels + 1):
        current = merge_bands(
            current, delay_tables, merge_level, device_pos * (channels_held >> merge_level)
        )
    merged_levels = local_levels
    if merged_levels < LEVELS:
        current = lax.all_gather(current, BANDS, axis=1, tiled=True)
        for merge_level in range(merged_levels + 1, LEVELS):
            current = merge_bands(current, delay_tables, merge_level, 0)
        dedispersed = own_trials(current, delay_tables, device_pos)
    else:
        dedispersed = current[:, 0]
    average = jnp.sum(dedispersed, axis=-1) / time_total
    deviation = dedispersed - average[..., None]
    spread = jnp.sum(deviation * deviation, axis=-1) / time_total
    inverse = lax.rsqrt(spread + EPSILON)
    scaled = deviation * inverse[..., None]
    scaled = lax.all_gather(scaled, "tm", axis=1, tiled=True)
    padded = jnp.pad(scaled, ((0, 0), (0, 0), (0, WMAX)))
    window = lax.dynamic_slice_in_dim(padded, time_pos * block_len, block_len + WMAX, 2)
    running = jnp.cumsum(jnp.pad(window, ((0, 0), (0, 0), (1, 0))), axis=-1)
    leading_sum = running[..., :block_len]
    filtered = []
    for width_index in range(box_widths.shape[0]):
        ending = lax.dynamic_slice_in_dim(running, box_widths[width_index], block_len, 2)
        filtered.append(ending - leading_sum)
    boxed = jnp.stack(filtered, axis=2)
    return boxed * lax.rsqrt(box_widths.astype(jnp.float32))[None, None, :, None]


def solution(mesh):
    in_specs = (P("beam", "freq", "tm"), P(), P())
    out_specs = P("beam", "freq", None, "tm")
    return jax.shard_map(body, mesh=mesh, in_specs=in_specs, out_specs=out_specs, check_vma=False)
```

profile of v0, /device:TPU:0, one launch (start us, length us, event | category | flops | bytes accessed | tf_op | source)
XLA Modules:
  0.0 143.2 jit_solution(5230237503584928580)
XLA Ops:
  6.5 1.9 %copy.33 = bf16[1,1024,256]{2,0,1:T(2,128)(2,1)S(1)} copy(bf16[1,1024,256]{2,1,0:T(8,128)(2,1)} %param.13) | data formatting | bytes 1048576 | tf_op args[0]
  8.4 0.5 broadcast.1330
  8.9 3.8 %reduce.32 = bf16[1024,256]{1,0:T(8,128)(2,1)S(1)} reduce(bf16[1024,1,256]{2,1,0:T(2,128)(2,1)S(1)} %bitcast.431, bf16[]{:T(256)} %broadcast.1330), dimensions={1}, to_apply=%bitcast.414.reduce_sub_computation | reduce | bytes 1048578
  12.7 0.9 reshape.1617
  13.6 3.5 %all-to-all-start = ((bf16[2,2,65536]{2,1,0:T(2,128)(2,1)}), bf16[2,2,65536]{2,1,0:T(2,128)(2,1)S(1)}, u32[]{:S(2)}, u32[]{:S(2)}) async-start(bf16[2,2,65536]{2,1,0:T(2,128)(2,1)} %reshape.1617), calls=%async_computation | async-start | bytes 1048576 | tf_op jit(solution)/shard_map/all_to_all | solution.py:109
  17.2 1.7 %all-to-all-done = bf16[2,2,65536]{2,1,0:T(2,128)(2,1)S(1)} async-done(((bf16[2,2,65536]{2,1,0:T(2,128)(2,1)}), bf16[2,2,65536]{2,1,0:T(2,128)(2,1)S(1)}, u32[]{:S(2)}, u32[]{:S(2)}) %all-to-all-start) | async-done | bytes 524320 | tf_op jit(solution)/shard_map/all_to_all | solution.py:109
  18.8 0.5 reshape.1618
  19.3 0.8 copy.32
  20.2 0.8 reshape.1235
  21.0 0.5 slice.414
  21.6 0.5 slice.417
  22.4 1.0 gather_fusion
  23.4 1.0 gather_fusion.1
  25.2 0.8 gather_fusion.2
  26.0 0.8 gather_fusion.3
  27.5 0.8 gather_fusion.4
  28.2 0.8 gather_fusion.5
  29.4 0.8 gather_fusion.7
  30.5 0.8 gather_fusion.6
  31.6 0.8 gather_fusion.9
  32.9 0.8 gather_fusion.8
  33.8 0.8 gather_fusion.11
  35.3 0.8 gather_fusion.10
  36.2 0.8 gather_fusion.13
  37.9 0.8 gather_fusion.12
  38.9 0.8 gather_fusion.15
  40.8 0.8 gather_fusion.14
  41.7 0.8 gather_fusion.17
  44.0 0.8 gather_fusion.16
  44.7 0.8 fusion.5
  45.6 0.7 fusion.79
  61.3 16.3 %all-gather.3.cloned.1.call-done = f32[8,128,512]{2,1,0:T(8,128)} async-done(((f32[1,128,512]{2,1,0:T(8,128)}), f32[8,128,512]{2,1,0:T(8,128)}) %all-gather.3.cloned.1.call-update) | async-done | bytes 2097168 | tf_op jit(solution)/shard_map/all_gather | solution.py:119
  77.6 1.8 %fusion.71 = (f32[1,4,128,512]{3,2,1,0:T(8,128)S(1)}, f32[1,4,128,512]{3,2,1,0:T(8,128)S(1)}) fusion(f32[1,8,128,512]{3,2,1,0:T(8,128)} %bitcast.434), kind=kLoop, calls=%fused_computation.354 | loop fusion | bytes 4194304 | tf_op jit(solution)/shard_map/slice | solution.py:53
  79.4 4.9 %gather_fusion.19 = f32[1024,512]{1,0:T(8,128)} fusion(f32[512,512]{1,0:T(8,128)S(1)} %bitcast.417, s32[1024]{0:T(1024)S(1)} %broadcast_clamp_fusion.2), kind=kCustom, calls=%fused_computation.20.clone | custom fusion | bytes 4198400 | tf_op jit(solution)/shard_map/jit(_take)/gather | solution.py:55
  84.3 1.8 %bitcast_select_fusion.2 = f32[1,1024,512]{2,1,0:T(8,128)S(1)} fusion(f32[1024,512]{1,0:T(8,128)} %gather_fusion.19, pred[1024]{0:T(1024)(128)(4,1)S(1)} %compare_and_fusion.2), kind=kLoop, calls=%fused_computation.27 | loop fusion | flops 524288 | bytes 4195328 | tf_op jit(solution)/shard_map/jit(_take)/select_n | solution.py:55
  86.1 0.6 slice.615
  86.7 1.0 copy-done
  87.7 1.2 pad_select_fusion.12
  88.9 0.6 slice.616
  89.8 0.6 slice.617
  90.7 0.6 slice.618
  91.6 0.6 slice.619
  92.5 0.6 slice.620
  93.3 2.0 %slice.621 = f32[1,1024,448]{2,1,0:T(8,128)} slice(f32[1,1024,512]{2,1,0:T(8,128)S(1)} %pad_select_fusion.7), slice={[0:1], [0:1024], [64:512]} | slice | bytes 3670016 | tf_op jit(solution)/shard_map/slice | solution.py:37
  95.3 4.9 %gather_fusion.18 = f32[1024,512]{1,0:T(8,128)} fusion(f32[512,512]{1,0:T(8,128)S(1)} %bitcast.416, s32[1024]{0:T(1024)S(1)} %broadcast_clamp_fusion.3), kind=kCustom, calls=%fused_computation.3.clone | custom fusion | bytes 4198400 | tf_op jit(solution)/shard_map/jit(_take)/gather | solution.py:54
  100.2 2.6 %fusion.1 = f32[1,1024,512]{2,1,0:T(8,128)S(1)} fusion(f32[1024,512]{1,0:T(8,128)} %gather_fusion.18, f32[1,1024,512]{2,1,0:T(8,128)S(1)} %pad_select_fusion.7, f32[1,1024,448]{2,1,0:T(8,128)} %slice.621, pred[1024]{0:T(1024)(128)(4,1)S(1)} %compare_and_fusion.3, pred[1024]{0:T(1024)(128)(4,1)S(1)} %get-tuple-element.18), kind=kLoop, calls=%fused_computation.29 | loop fusion | flops 1572864 | bytes 8128512 | tf_op jit(solution)/shard_map/add | solution.py:57
  102.9 4.9 %gather_fusion.21 = f32[1024,512]{1,0:T(8,128)} fusion(f32[512,512]{1,0:T(8,128)S(1)} %bitcast.418, s32[1024]{0:T(1024)S(1)} %broadcast_clamp_fusion), kind=kCustom, calls=%fused_computation.22.clone | custom fusion | bytes 4198400 | tf_op jit(solution)/shard_map/jit(_take)/gather | solution.py:55
  107.8 1.8 %bitcast_select_fusion = f32[1,1024,512]{2,1,0:T(8,128)S(1)} fusion(f32[1024,512]{1,0:T(8,128)} %gather_fusion.21, pred[1024]{0:T(1024)(128)(4,1)S(1)} %compare_and_fusion), kind=kLoop, calls=%fused_computation.24 | loop fusion | flops 524288 | bytes 4195328 | tf_op jit(solution)/shard_map/jit(_take)/select_n | solution.py:55
  109.6 0.6 slice.624
  110.2 1.0 copy-done.1
  111.2 1.3 pad_select_fusion.6
  112.5 0.6 slice.625
  113.4 0.6 slice.626
  114.2 0.6 slice.627
  115.1 0.6 slice.628
  116.0 0.6 slice.629
  116.9 0.6 slice.630
  117.8 1.3 slice.631
  119.1 4.9 %gather_fusion.20 = f32[1024,512]{1,0:T(8,128)} fusion(f32[512,512]{1,0:T(8,128)S(1)} %bitcast.415, s32[1024]{0:T(1024)S(1)} %broadcast_clamp_fusion.1), kind=kCustom, calls=%fused_computation.21.clone | custom fusion | bytes 4198400 | tf_op jit(solution)/shard_map/jit(_take)/gather | solution.py:54
  123.9 2.4 %fusion = f32[1,1024,512]{2,1,0:T(8,128)S(1)} fusion(f32[1024,512]{1,0:T(8,128)} %gather_fusion.20, f32[1,1024,512]{2,1,0:T(8,128)S(1)} %pad_select_fusion, f32[1,1024,384]{2,1,0:T(8,128)} %slice.631, pred[1024]{0:T(1024)(128)(4,1)S(1)} %compare_and_fusion.1, pred[1024]{0:T(1024)(128)(4,1)S(1)} %get-tuple-element.6), kind=kLoop, calls=%fused_computation.26 | loop fusion | flops 1572864 | bytes 7866368 | tf_op jit(solution)/shard_map/add | solution.py:57
  126.5 0.8 gather_fusion.23
  129.2 0.8 gather_fusion.22
  130.4 2.2 %all_gather.7 = f32[1,256,512]{2,1,0:T(8,128)S(1)} all-gather(f32[1,128,512]{2,1,0:T(8,128)S(1)} %subtract_multiply_fusion), channel_id=1, replica_groups=mesh['freq'=4,'tm'=2,'beam'=4] {'tm'}, dimensions={1}, use_global_device_ids=true | all-gather | bytes 786432 | tf_op jit(solution)/shard_map/all_gather | solution.py:130
  134.4 2.0 %copy.25 = f32[1,256,8,256]{3,2,1,0:T(8,128)} copy(f32[1,256,8,256]{1,3,2,0:T(8,128)S(1)} %broadcast_multiply_fusion) | data formatting | bytes 4194304 | tf_op jit(solution)/shard_map/mul | solution.py:140
  (181 shorter events, 15.4 us)
Async XLA Ops:
  13.6 5.2 %all-to-all-start = ((bf16[2,2,65536]{2,1,0:T(2,128)(2,1)}), bf16[2,2,65536]{2,1,0:T(2,128)(2,1)S(1)}, u32[]{:S(2)}, u32[]{:S(2)}) async-start(bf16[2,2,65536]{2,1,0:T(2,128)(2,1)} %reshape.1617), calls=%async_computation | async-start | bytes 1048576 | tf_op jit(solution)/shard_map/all_to_all | solution.py:109
  17.1 60.5 %all-gather.3.cloned.1.call-start = ((), (), s32[]{:S(2)}) async-start(), calls=%async_computation.1 | async-start | bytes 2359296 | tf_op jit(solution)/shard_map/all_gather | solution.py:119
  20.1 2.0 %copy-start.2 = (s32[3,12,2048]{2,1,0:T(8,128)S(1)}, s32[3,12,2048]{2,1,0:T(8,128)}, u32[]{:S(2)}) copy-start(s32[3,12,2048]{2,1,0:T(8,128)} %param.14) | copy-start | bytes 884740
  43.8 1.8 %copy-start.3 = (s32[8]{0:T(128)S(1)}, s32[8]{0:T(128)}, u32[]{:S(2)}) copy-start(s32[8]{0:T(128)} %param.15) | copy-start | bytes 100
  86.1 1.6 %copy-start = (f32[1024,512]{1,0:T(8,128)S(1)}, f32[1024,512]{1,0:T(8,128)}, u32[]{:S(2)}) copy-start(f32[1024,512]{1,0:T(8,128)} %gather_fusion.19) | copy-start | bytes 6291460
  109.6 1.6 %copy-start.1 = (f32[1024,512]{1,0:T(8,128)S(1)}, f32[1024,512]{1,0:T(8,128)}, u32[]{:S(2)}) copy-start(f32[1024,512]{1,0:T(8,128)} %gather_fusion.21) | copy-start | bytes 6291460
Sparse Core Ops, SparseCore 0:
  45.7 31.8 all-gather.2
where the time goes:
time: 144 us; the launch traced here: 143 us
  local copies, waits for them, and re-layouts  65.7 us (46%)
  between operations  29.5 us (20%)
  other arithmetic  24.3 us (17%)
  waiting for transfers between devices  18 us (12%)
  starting transfers between devices  3.53 us (2%)
  blocking collectives  2.18 us (2%)
    gather x11, local copies, waits for them, and re-layouts, merge_bands(): chosen = jnp.take(upper_flat, band_base + entries[1], axis=1)  16.8 us
    gather x11, local copies, waits for them, and re-layouts, merge_bands(): picked = jnp.take(lower_flat, band_base + entries[0], axis=1)  16.8 us
    all_gather x1, waiting for transfers between devices, body(): current = lax.all_gather(current, BANDS, axis=1, tiled=True)  16.3 us
    slice x45, local copies, waits for them, and re-layouts, shift_rows(): result[..., step_size:]  14.7 us
    select_n x36, other arithmetic, shift_rows(): result = jnp.where(flag[None, :, None], moved, result)  7.66 us
    add x8, other arithmetic, merge_bands(): return (picked + delayed).reshape(beam_count, bands_out, depth_out, columns)  6.29 us
    unnamed x12, local copies, waits for them, and re-layouts  5.69 us
    unnamed x8, other arithmetic  4.18 us
  transfers between devices with their start and end apart: 2, of which 2 were waited for; matrix products, arithmetic and copies ran while one was open for 1% of the time, Pallas kernels for 0%

commit v1 on v0

--- a/solution.py
+++ b/solution.py
@@ -106,7 +106,10 @@
     time_pos = lax.axis_index("tm")
     device_pos = lax.axis_index("freq") * time_parts + time_pos
     block_len = intensity.shape[2]
-    whole_rows = lax.all_to_all(intensity, "tm", 1, 2, tiled=True)
+    whole_rows = jnp.concatenate(
+        lax.all_to_all(jnp.stack(jnp.split(intensity, lax.axis_size("tm"), axis=1)), "tm", 0, 0),
+        axis=2,
+    )
     beam_count, channels_held, time_total = whole_rows.shape
     local_levels = channels_held.bit_length() - 1
     current = whole_rows.astype(jnp.float32)[:, :, None, :]

time: 144 us -> 138 us (0.958)
  other arithmetic: 24.3 us -> 21.3 us
  local copies, waits for them, and re-layouts: 65.7 us -> 62.9 us
    unnamed x8 -> x7, other arithmetic: 4.18 us -> 0.36 us
    unnamed x12 -> x8, local copies, waits for them, and re-layouts: 5.69 us -> 1.97 us
where the time goes in v1:
time: 138 us; the launch traced here: 137 us
  local copies, waits for them, and re-layouts  62.9 us (46%)
  between operations  29.5 us (21%)
  other arithmetic  21.3 us (15%)
  waiting for transfers between devices  18 us (13%)
  starting transfers between devices  3.53 us (3%)
  blocking collectives  2.18 us (2%)
    gather x11, local copies, waits for them, and re-layouts, merge_bands(): chosen = jnp.take(upper_flat, band_base + entries[1], axis=1)  16.8 us
    gather x11, local copies, waits for them, and re-layouts, merge_bands(): picked = jnp.take(lower_flat, band_base + entries[0], axis=1)  16.8 us
    all_gather x1, waiting for transfers between devices, body(): current = lax.all_gather(current, BANDS, axis=1, tiled=True)  16.3 us
    slice x45, local copies, waits for them, and re-layouts, shift_rows(): result[..., step_size:]  14.7 us
    select_n x36, other arithmetic, shift_rows(): result = jnp.where(flag[None, :, None], moved, result)  7.57 us
    add x8, other arithmetic, merge_bands(): return (picked + delayed).reshape(beam_count, bands_out, depth_out, columns)  6.29 us
    select_n x9, other arithmetic, merge_bands(): chosen = jnp.take(upper_flat, band_base + entries[1], axis=1)  4.13 us
    all_to_all x1, starting transfers between devices, body(): lax.all_to_all(jnp.stack(jnp.split(intensity, lax.axis_size('tm'), axis=1...  3.49 us
  transfers between devices with their start and end apart: 2, of which 2 were waited for; matrix products, arithmetic and copies ran while one was open for 1% of the time, Pallas kernels for 0%

profile of v1, /device:TPU:0, one launch (start us, length us, event | category | flops | bytes accessed | tf_op | source)
XLA Modules:
  0.0 137.3 jit_solution(16406924316088087563)
XLA Ops:
  6.5 1.1 slice_bitcast_fusion.3
  7.6 0.8 pad_maximum_fusion
  8.4 3.5 %all-to-all-start = ((bf16[2,1,512,256]{3,2,1,0:T(8,128)(2,1)}), bf16[2,1,512,256]{3,2,1,0:T(8,128)(2,1)S(1)}, u32[]{:S(2)}, u32[]{:S(2)}) async-start(bf16[2,1,512,256]{3,2,1,0:T(8,128)(2,1)} %pad_maximum_fusion), calls=%async_computation | async-start | bytes 1048576 | tf_op jit(solution)/shard_map/all_to_all | solution.py:110
  12.0 1.7 %all-to-all-done = bf16[2,1,512,256]{3,2,1,0:T(8,128)(2,1)S(1)} async-done(((bf16[2,1,512,256]{3,2,1,0:T(8,128)(2,1)}), bf16[2,1,512,256]{3,2,1,0:T(8,128)(2,1)S(1)}, u32[]{:S(2)}, u32[]{:S(2)}) %all-to-all-start) | async-done | bytes 524320 | tf_op jit(solution)/shard_map/all_to_all | solution.py:110
  13.7 0.8 copy.21
  14.6 0.8 reshape.1235
  15.4 0.5 slice.414
  16.0 0.5 slice.417
  16.8 1.0 gather_fusion
  17.8 1.0 gather_fusion.1
  18.9 0.3 slice.419
  19.3 0.3 slice.422
  19.6 0.8 gather_fusion.2
  20.4 0.8 gather_fusion.3
  21.7 0.8 gather_fusion.4
  22.5 0.8 gather_fusion.5
  23.7 0.8 gather_fusion.7
  24.8 0.8 gather_fusion.6
  25.8 0.8 gather_fusion.9
  27.1 0.8 gather_fusion.8
  28.0 0.8 gather_fusion.11
  29.5 0.8 gather_fusion.10
  30.4 0.8 gather_fusion.13
  32.2 0.8 gather_fusion.12
  33.1 0.8 gather_fusion.15
  35.1 0.8 gather_fusion.14
  36.0 0.8 gather_fusion.17
  38.2 0.8 gather_fusion.16
  39.0 0.8 fusion.5
  39.8 0.7 fusion.79
  55.6 16.3 %all-gather.3.cloned.1.call-done = f32[8,128,512]{2,1,0:T(8,128)} async-done(((f32[1,128,512]{2,1,0:T(8,128)}), f32[8,128,512]{2,1,0:T(8,128)}) %all-gather.3.cloned.1.call-update) | async-done | bytes 2097168 | tf_op jit(solution)/shard_map/all_gather | solution.py:122
  71.8 1.8 %fusion.71 = (f32[1,4,128,512]{3,2,1,0:T(8,128)S(1)}, f32[1,4,128,512]{3,2,1,0:T(8,128)S(1)}) fusion(f32[1,8,128,512]{3,2,1,0:T(8,128)} %bitcast.428), kind=kLoop, calls=%fused_computation.357 | loop fusion | bytes 4194304 | tf_op jit(solution)/shard_map/slice | solution.py:53
  73.7 4.9 %gather_fusion.19 = f32[1024,512]{1,0:T(8,128)} fusion(f32[512,512]{1,0:T(8,128)S(1)} %bitcast.414, s32[1024]{0:T(1024)S(1)} %broadcast_clamp_fusion.2), kind=kCustom, calls=%fused_computation.20.clone | custom fusion | bytes 4198400 | tf_op jit(solution)/shard_map/jit(_take)/gather | solution.py:55
  78.5 1.8 %bitcast_select_fusion.2 = f32[1,1024,512]{2,1,0:T(8,128)S(1)} fusion(f32[1024,512]{1,0:T(8,128)} %gather_fusion.19, pred[1024]{0:T(1024)(128)(4,1)S(1)} %compare_and_fusion.2), kind=kLoop, calls=%fused_computation.27 | loop fusion | flops 524288 | bytes 4195328 | tf_op jit(solution)/shard_map/jit(_take)/select_n | solution.py:55
  80.4 0.6 slice.615
  81.0 1.0 copy-done
  81.9 1.2 pad_select_fusion.12
  83.1 0.6 slice.616
  84.0 0.6 slice.617
  84.9 0.6 slice.618
  85.8 0.6 slice.619
  86.7 0.6 slice.620
  87.5 2.0 %slice.621 = f32[1,1024,448]{2,1,0:T(8,128)} slice(f32[1,1024,512]{2,1,0:T(8,128)S(1)} %pad_select_fusion.7), slice={[0:1], [0:1024], [64:512]} | slice | bytes 3670016 | tf_op jit(solution)/shard_map/slice | solution.py:37
  89.5 4.9 %gather_fusion.18 = f32[1024,512]{1,0:T(8,128)} fusion(f32[512,512]{1,0:T(8,128)S(1)} %bitcast.413, s32[1024]{0:T(1024)S(1)} %broadcast_clamp_fusion.3), kind=kCustom, calls=%fused_computation.3.clone | custom fusion | bytes 4198400 | tf_op jit(solution)/shard_map/jit(_take)/gather | solution.py:54
  94.4 2.6 %fusion.1 = f32[1,1024,512]{2,1,0:T(8,128)S(1)} fusion(f32[1024,512]{1,0:T(8,128)} %gather_fusion.18, f32[1,1024,512]{2,1,0:T(8,128)S(1)} %pad_select_fusion.7, f32[1,1024,448]{2,1,0:T(8,128)} %slice.621, pred[1024]{0:T(1024)(128)(4,1)S(1)} %compare_and_fusion.3, pred[1024]{0:T(1024)(128)(4,1)S(1)} %get-tuple-element.18), kind=kLoop, calls=%fused_computation.29 | loop fusion | flops 1572864 | bytes 8128512 | tf_op jit(solution)/shard_map/add | solution.py:57
  97.1 4.9 %gather_fusion.21 = f32[1024,512]{1,0:T(8,128)} fusion(f32[512,512]{1,0:T(8,128)S(1)} %bitcast.415, s32[1024]{0:T(1024)S(1)} %broadcast_clamp_fusion), kind=kCustom, calls=%fused_computation.22.clone | custom fusion | bytes 4198400 | tf_op jit(solution)/shard_map/jit(_take)/gather | solution.py:55
  102.0 1.8 %bitcast_select_fusion = f32[1,1024,512]{2,1,0:T(8,128)S(1)} fusion(f32[1024,512]{1,0:T(8,128)} %gather_fusion.21, pred[1024]{0:T(1024)(128)(4,1)S(1)} %compare_and_fusion), kind=kLoop, calls=%fused_computation.24 | loop fusion | flops 524288 | bytes 4195328 | tf_op jit(solution)/shard_map/jit(_take)/select_n | solution.py:55
  103.8 0.6 slice.624
  104.4 1.0 copy-done.1
  105.4 1.2 pad_select_fusion.6
  106.6 0.6 slice.625
  107.5 0.6 slice.626
  108.1 0.3 pad_select_fusion.4
  108.4 0.6 slice.627
  109.3 0.6 slice.628
  110.2 0.6 slice.629
  111.0 0.6 slice.630
  111.9 1.3 slice.631
  113.2 4.9 %gather_fusion.20 = f32[1024,512]{1,0:T(8,128)} fusion(f32[512,512]{1,0:T(8,128)S(1)} %bitcast.412, s32[1024]{0:T(1024)S(1)} %broadcast_clamp_fusion.1), kind=kCustom, calls=%fused_computation.21.clone | custom fusion | bytes 4198400 | tf_op jit(solution)/shard_map/jit(_take)/gather | solution.py:54
  118.1 2.4 %fusion = f32[1,1024,512]{2,1,0:T(8,128)S(1)} fusion(f32[1024,512]{1,0:T(8,128)} %gather_fusion.20, f32[1,1024,512]{2,1,0:T(8,128)S(1)} %pad_select_fusion, f32[1,1024,384]{2,1,0:T(8,128)} %slice.631, pred[1024]{0:T(1024)(128)(4,1)S(1)} %compare_and_fusion.1, pred[1024]{0:T(1024)(128)(4,1)S(1)} %get-tuple-element.6), kind=kLoop, calls=%fused_computation.26 | loop fusion | flops 1572864 | bytes 7866368 | tf_op jit(solution)/shard_map/add | solution.py:57
  120.7 0.8 gather_fusion.23
  123.3 0.8 gather_fusion.22
  124.6 2.2 %all_gather.7 = f32[1,256,512]{2,1,0:T(8,128)S(1)} all-gather(f32[1,128,512]{2,1,0:T(8,128)S(1)} %subtract_multiply_fusion), channel_id=1, replica_groups=mesh['freq'=4,'tm'=2,'beam'=4] {'tm'}, dimensions={1}, use_global_device_ids=true | all-gather | bytes 786432 | tf_op jit(solution)/shard_map/all_gather | solution.py:133
  128.5 2.0 %copy.24 = f32[1,256,8,256]{3,2,1,0:T(8,128)} copy(f32[1,256,8,256]{1,3,2,0:T(8,128)S(1)} %broadcast_multiply_fusion) | data formatting | bytes 4194304 | tf_op jit(solution)/shard_map/mul | solution.py:143
  (179 shorter events, 14.4 us)
Async XLA Ops:
  8.4 5.2 %all-to-all-start = ((bf16[2,1,512,256]{3,2,1,0:T(8,128)(2,1)}), bf16[2,1,512,256]{3,2,1,0:T(8,128)(2,1)S(1)}, u32[]{:S(2)}, u32[]{:S(2)}) async-start(bf16[2,1,512,256]{3,2,1,0:T(8,128)(2,1)} %pad_maximum_fusion), calls=%async_computation | async-start | bytes 1048576 | tf_op jit(solution)/shard_map/all_to_all | solution.py:110
  11.9 59.9 %all-gather.3.cloned.1.call-start = ((), (), s32[]{:S(2)}) async-start(), calls=%async_computation.1 | async-start | bytes 2359296 | tf_op jit(solution)/shard_map/all_gather | solution.py:122
  14.6 2.0 %copy-start.2 = (s32[3,12,2048]{2,1,0:T(8,128)S(1)}, s32[3,12,2048]{2,1,0:T(8,128)}, u32[]{:S(2)}) copy-start(s32[3,12,2048]{2,1,0:T(8,128)} %param.14) | copy-start | bytes 884740
  38.0 1.8 %copy-start.3 = (s32[8]{0:T(128)S(1)}, s32[8]{0:T(128)}, u32[]{:S(2)}) copy-start(s32[8]{0:T(128)} %param.15) | copy-start | bytes 100
  80.3 1.6 %copy-start = (f32[1024,512]{1,0:T(8,128)S(1)}, f32[1024,512]{1,0:T(8,128)}, u32[]{:S(2)}) copy-start(f32[1024,512]{1,0:T(8,128)} %gather_fusion.19) | copy-start | bytes 6291460
  103.8 1.6 %copy-start.1 = (f32[1024,512]{1,0:T(8,128)S(1)}, f32[1024,512]{1,0:T(8,128)}, u32[]{:S(2)}) copy-start(f32[1024,512]{1,0:T(8,128)} %gather_fusion.21) | copy-start | bytes 6291460
Sparse Core Ops, SparseCore 0:
  39.9 31.8 all-gather.2
